TPU v7x, 256 devices: a whole 4x4x8 slice. The times are simulated.
256 devices in a mesh: cfg: 2 (over core), req: 8 (over z), seq: 16 (over y, x).
Axes of the slice: x: 4, y: 4, z: 8, core: 2. Of those that a mesh axis runs over, the one named last changes fastest.
Arguments:
- queries: bfloat16 [2, 8, 768, 1536], P('cfg', 'req', 'seq'), may hold values from -50 to 50
- text_cache: bfloat16 [2, 8, 2, 512, 1536], P('cfg', 'req'), may hold values from -6 to 6
- image_cache: bfloat16 [2, 8, 2, 768, 1536], P('cfg', 'req'), may hold values from -6 to 6
- fresh_kv: bfloat16 [2, 8, 2, 96, 1536], P('cfg', 'req', None, 'seq'), may hold values from -6 to 6
- fresh_slots: int32 [8, 96], P('req'), may hold values from 0 to 767, as said below
- fresh_pos: int32 [3, 8, 96], P(None, 'req', 'seq'), may hold values from 0 to 63
- image_len: int32 [8], replicated, may hold values from 384 to 768, as said below
- stream: bfloat16 [2, 8, 768, 3072], P('cfg', None, 'seq', 'req'), may hold values from -30 to 30
- modulation: float32 [2, 8, 4, 3072], replicated, may hold values from -4 to 4
- out_weight: bfloat16 [1536, 3072], P('seq', 'req'), may hold values from -0.15625 to 0.15625
- up_weight: bfloat16 [3072, 12288], P('seq', 'req'), may hold values from -0.109375 to 0.109375
- down_weight: bfloat16 [12288, 3072], P('req', 'seq'), may hold values from -0.0546875 to 0.0546875
- final_weight: bfloat16 [3072, 64], replicated, may hold values from -0.109375 to 0.109375
- latent: float32 [8, 384, 128], P('req', 'seq', 'cfg'), may hold values from -6 to 6
- step_index: int32 [1], replicated, may hold values from 0 to 27
Outputs:
- latent_next: float32 [8, 384, 128], P('req', 'seq', 'cfg')
- denoised: float32 [8, 384, 128], P('req', 'seq', 'cfg')
Inputs may be any that keep to these rules, and one draw needn't show every extreme that they name: `fresh_slots`: columns k * 6 to (k + 1) * 6 - 1 of a row hold distinct slots from k * 48 to (k + 1) * 48 - 1. `image_len`: some request has exactly 768 image tokens and some other exactly 384.
All inputs are finite; a program needn't handle non-finite values.
Results may differ from a plain program's by a relative error of at most 0.0095.
Values may be sent and summed in bfloat16 or wider, within the bound.
A program may use at most 128 MiB of HBM per device.

v0:
```python
import math
import jax
import jax.numpy as jnp
from jax import lax
from jax.sharding import PartitionSpec as P

STEPS = 28
GUIDANCE = 3.0
SHIFT = 3.0
SCALE = 1.0 / math.sqrt(128.0)
EPSILON = 1e-06


def swapped(block, axis, stride):
    count = lax.axis_size(axis)
    route = []
    for low in range(count):
        high = low | 1 << stride
        if high != low and high < count:
            route += [(low, high), (high, low)]
    return lax.ppermute(block, axis, route)


def rope_angles(positions):
    columns = []
    for component, axis_span in ((0, 16), (1, 56), (2, 56)):
        pair_ids = jnp.arange(axis_span // 2, dtype=jnp.float32)
        frequency = jnp.exp(-(2.0 * pair_ids / axis_span) * math.log(10000.0))
        columns.append(positions[component].astype(jnp.float32)[:, None] * frequency[None, :])
    return jnp.concatenate(columns, axis=1)


def rotate(key_rows, angles):
    row_total = key_rows.shape[0]
    paired = key_rows.reshape(row_total, -1, 64, 2)
    cosine = jnp.cos(angles)[:, None, :]
    sine = jnp.sin(angles)[:, None, :]
    first = cosine * paired[..., 0] - sine * paired[..., 1]
    second = sine * paired[..., 0] + cosine * paired[..., 1]
    return jnp.stack([first, second], axis=-1).reshape(row_total, -1)


def noise_level(index):
    fraction = 1.0 - index.astype(jnp.float32) / STEPS
    return SHIFT * fraction / (SHIFT * fraction + 1.0 - fraction)


def head_scores(query_heads, key_rows):
    key_heads = key_rows.reshape(key_rows.shape[0], -1, 128)
    return (
        jnp.einsum("qhd,khd->hqk", query_heads, key_heads, preferred_element_type=jnp.float32)
        * SCALE
    )


def head_mix(weights, value_rows):
    value_heads = value_rows.reshape(value_rows.shape[0], -1, 128)
    return jnp.einsum("hqk,khd->qhd", weights, value_heads, preferred_element_type=jnp.float32)


def per_device(
    queries,
    text_cache,
    image_cache,
    fresh_kv,
    fresh_slots,
    fresh_pos,
    image_len,
    stream,
    modulation,
    out_weight,
    up_weight,
    down_weight,
    final_weight,
    latent,
    step_index,
):
    cfg_id = lax.axis_index("cfg")
    req_id = lax.axis_index("req")
    seq_id = lax.axis_index("seq")
    query_rows = queries[0, 0]
    row_count = query_rows.shape[0]
    query_heads = query_rows.reshape(row_count, -1, 128)
    text_kv = text_cache[0, 0]
    image_kv = image_cache[0, 0]
    angles = rope_angles(fresh_pos[:, 0, :])
    fresh_keys = rotate(fresh_kv[0, 0, 0].astype(jnp.float32), angles).astype(jnp.bfloat16)
    fresh_pair = jnp.stack([fresh_keys, fresh_kv[0, 0, 1]], axis=0)
    all_fresh, proj_cols, up_cols, down_rows = (
        lax.all_gather(fresh_pair, "seq", axis=1, tiled=True),
        lax.all_gather(out_weight, "seq", axis=0, tiled=True),
        lax.all_gather(up_weight, "seq", axis=0, tiled=True),
        lax.all_gather(down_weight, "seq", axis=1, tiled=True),
    )
    image_kv = image_kv.at[:, fresh_slots[0], :].set(all_fresh)
    length = lax.dynamic_index_in_dim(image_len, req_id, 0, keepdims=False)
    image_total = image_kv.shape[1]
    text_scores = head_scores(query_heads, text_kv[0])
    text_best = jnp.max(text_scores, axis=-1, keepdims=True)
    live_keys = (jnp.arange(image_total) < length)[None, None, :]
    image_scores = jnp.where(live_keys, head_scores(query_heads, image_kv[0]), -jnp.inf)
    row_max = jnp.maximum(text_best, jnp.max(image_scores, axis=-1, keepdims=True))
    text_probs = jnp.exp(text_scores - row_max)
    image_probs = jnp.exp(image_scores - row_max)
    total = jnp.sum(text_probs, axis=-1) + jnp.sum(image_probs, axis=-1)
    mixed = head_mix(text_probs.astype(jnp.bfloat16), text_kv[1]) + head_mix(
        image_probs.astype(jnp.bfloat16), image_kv[1]
    )
    attended = (
        (mixed / jnp.transpose(total)[:, :, None]).reshape(row_count, -1).astype(jnp.bfloat16)
    )
    projected = jnp.dot(
        lax.all_gather(attended, "req", axis=0, tiled=True),
        proj_cols,
        preferred_element_type=jnp.float32,
    )
    requests = stream.shape[1]
    col_count = stream.shape[3]
    mod_half = lax.dynamic_index_in_dim(modulation, cfg_id, 0, keepdims=False)
    gate_cols = lax.dynamic_slice_in_dim(mod_half[:, 0, :], req_id * col_count, col_count, 1)
    residual = (
        stream[0].astype(jnp.float32)
        + gate_cols[:, None, :] * projected.reshape(requests, row_count, col_count)
    ).astype(jnp.bfloat16)
    full_rows = lax.all_gather(
        residual.reshape(requests * row_count, col_count), "req", axis=1, tiled=True
    )
    wide = full_rows.reshape(requests, row_count, -1).astype(jnp.float32)
    average = jnp.mean(wide, axis=-1, keepdims=True)
    centered = wide - average
    spread = jnp.mean(centered * centered, axis=-1, keepdims=True)
    normed = (
        centered * lax.rsqrt(spread + EPSILON) * (1.0 + mod_half[:, 2][:, None, :])
        + mod_half[:, 1][:, None, :]
    )
    normed = normed.astype(jnp.bfloat16).reshape(requests * row_count, -1)

    def rows_product(left_rows, right):
        return jnp.dot(left_rows, right, preferred_element_type=jnp.float32)

    pre_act = rows_product(normed, up_cols)
    activated = jax.nn.gelu(pre_act, approximate=True).astype(jnp.bfloat16)
    mlp_rows = lax.psum_scatter(
        rows_product(activated, down_rows).astype(jnp.bfloat16),
        "req",
        scatter_dimension=0,
        tiled=True,
    ).astype(jnp.float32)
    own_rows = lax.dynamic_slice_in_dim(full_rows, req_id * row_count, row_count, 0)
    gate_two = lax.dynamic_index_in_dim(mod_half[:, 3, :], req_id, 0, keepdims=False)
    block_out = (own_rows.astype(jnp.float32) + gate_two[None, :] * mlp_rows).astype(jnp.bfloat16)
    velocity = jnp.dot(block_out, final_weight, preferred_element_type=jnp.float32).reshape(
        row_count // 2, -1
    )
    lane_count = velocity.shape[1]
    half_lanes = lane_count // 2
    outgoing = lax.dynamic_slice_in_dim(velocity, (1 - cfg_id) * half_lanes, half_lanes, 1)
    own_part = lax.dynamic_slice_in_dim(velocity, cfg_id * half_lanes, half_lanes, 1)
    partner = swapped(outgoing, "cfg", 0)
    cond_part = jnp.where(cfg_id == 0, own_part, partner)
    uncond_part = jnp.where(cfg_id == 0, partner, own_part)
    guided = uncond_part + GUIDANCE * (cond_part - uncond_part)
    level_now = noise_level(step_index[0])
    level_next = noise_level(step_index[0] + 1)
    token_ids = (
        seq_id * row_count
        + 2 * jnp.arange(row_count // 2, dtype=jnp.int32)[:, None]
        + cfg_id
        + jnp.zeros((1, half_lanes), jnp.int32)
    )
    valid = token_ids < length
    current = latent[0]
    latent_next = jnp.where(valid, current + (level_next - level_now) * guided, current)
    denoised = jnp.where(valid, current - level_now * guided, current)
    return (latent_next[None], denoised[None])


def solution(mesh):
    in_specs = (
        P("cfg", "req", "seq", None),
        P("cfg", "req", None, None, None),
        P("cfg", "req", None, None, None),
        P("cfg", "req", None, "seq", None),
        P("req", None),
        P(None, "req", "seq"),
        P(),
        P("cfg", None, "seq", "req"),
        P(),
        P("seq", "req"),
        P("seq", "req"),
        P("req", "seq"),
        P(),
        P("req", "seq", "cfg"),
        P(),
    )
    out_specs = (P("req", "seq", "cfg"), P("req", "seq", "cfg"))
    return jax.shard_map(
        per_device, mesh=mesh, in_specs=in_specs, out_specs=out_specs, check_vma=False
    )
```

profile of v0, /device:TPU:1, one launch (start us, length us, event | category | flops | bytes accessed | tf_op | source)
XLA Modules:
  0.0 484.3 jit_solution(10954910353682535081)
XLA Ops:
  8.5 0.9 fusion.58
  9.7 1.0 multiply_subtract_fusion
  12.5 20.3 %all_gather.18 = bf16[2,96,1536]{2,0,1:T(2,128)(2,1)S(1)} all-gather(bf16[2,6,1536]{2,0,1:T(2,128)(2,1)S(1)} %pad_maximum_fusion.1), channel_id=1, replica_groups=mesh['cfg'=2,'req'=8,'seq'=16] {'seq'}, dimensions={1}, use_global_device_ids=true | all-gather | bytes 626688 | tf_op jit(solution)/shard_map/all_gather | solution.py:90
  32.8 9.4 %copy.107 = bf16[1,1,2,768,1536]{4,2,3,1,0:T(2,128)(2,1)} copy(bf16[1,1,2,768,1536]{4,3,2,1,0:T(8,128)(2,1)} %param.17) | data formatting | bytes 9437184 | tf_op args[2]
  42.2 11.7 %scatter_fusion = bf16[2,768,1536]{2,0,1:T(2,128)(2,1)} fusion(bf16[2,768,1536]{2,0,1:T(2,128)(2,1)} %bitcast.99, s32[96]{0:T(128)S(1)} %fusion.46, bf16[96,2,1536]{2,1,0:T(2,128)(2,1)S(1)} %bitcast.106), kind=kCustom, calls=%fused_computation | custom fusion | bytes 1769856 | tf_op jit(solution)/shard_map/scatter | solution.py:95
  53.9 10.7 %fusion.55 = (bf16[1,768,1536]{2,0,1:T(2,128)(2,1)}, bf16[1,768,1536]{2,0,1:T(2,128)(2,1)}) fusion(bf16[2,768,1536]{2,0,1:T(2,128)(2,1)} %scatter_fusion), kind=kLoop, calls=%fused_computation.100 | loop fusion | bytes 9437184 | tf_op jit(solution)/shard_map/slice | solution.py:107
  64.6 11.7 %copy.72 = bf16[1,768,1536]{1,2,0:T(8,128)(2,1)} copy(bf16[1,768,1536]{2,0,1:T(2,128)(2,1)} %get-tuple-element.3) | data formatting | bytes 4718592 | tf_op jit(solution)/shard_map/slice | solution.py:101
  77.6 0.8 reshape_squeeze.15
  78.4 3.7 fusion.56
  82.2 1.7 copy.87
  83.9 1.5 fusion.59
  86.3 1.3 copy-done.4
  87.6 1.2 fusion.15
  88.7 1.0 fusion.28
  89.7 1.7 copy.90
  91.4 1.5 convolution_bitcast_fusion.1
  92.9 11.8 %copy.77 = bf16[1,768,1536]{1,2,0:T(8,128)(2,1)} copy(bf16[1,768,1536]{2,0,1:T(2,128)(2,1)} %get-tuple-element.2) | data formatting | bytes 4718592 | tf_op jit(solution)/shard_map/slice | solution.py:107
  104.8 2.7 fusion.27
  109.3 0.9 fusion.57
  110.2 39.1 %all-gather.6.cloned.1.call-done = bf16[384,1536]{1,0:T(8,128)(2,1)} async-done(((bf16[48,1536]{1,0:T(8,128)(2,1)}), bf16[384,1536]{1,0:T(8,128)(2,1)}) %all-gather.6.cloned.1.call-update) | async-done | bytes 1179664 | tf_op jit(solution)/shard_map/all_gather | solution.py:113
  149.3 52.0 %all-gather.8.cloned.1.call-done = bf16[1536,384]{1,0:T(8,128)(2,1)} async-done(((bf16[96,384]{1,0:T(8,128)(2,1)}), bf16[1536,384]{1,0:T(8,128)(2,1)}) %all-gather.8.cloned.1.call-update) | async-done | bytes 1179664 | tf_op jit(solution)/shard_map/all_gather | solution.py:91
  201.4 3.1 fusion.18
  205.8 38.7 %all-gather.10.cloned.1.call-done = bf16[384,3072]{1,0:T(8,128)(2,1)} async-done(((bf16[384,384]{1,0:T(8,128)(2,1)}), bf16[384,3072]{1,0:T(8,128)(2,1)}) %all-gather.10.cloned.1.call-update) | async-done | bytes 2359312 | tf_op jit(solution)/shard_map/all_gather | solution.py:125
  244.5 2.2 convert_reduce_fusion
  247.6 2.6 fusion.5
  250.3 78.9 %all-gather.12.cloned.1.call-done = bf16[3072,1536]{1,0:T(8,128)(2,1)} async-done(((bf16[192,1536]{1,0:T(8,128)(2,1)}), bf16[3072,1536]{1,0:T(8,128)(2,1)}) %all-gather.12.cloned.1.call-update) | async-done | bytes 9437200 | tf_op jit(solution)/shard_map/all_gather | solution.py:92
  329.2 82.8 %all-gather.14.cloned.1.call-done = bf16[1536,3072]{0,1:T(8,128)(2,1)} async-done(((bf16[1536,192]{0,1:T(8,128)(2,1)}), bf16[1536,3072]{0,1:T(8,128)(2,1)}) %all-gather.14.cloned.1.call-update) | async-done | bytes 9437200 | tf_op jit(solution)/shard_map/all_gather | solution.py:93
  412.0 16.2 %convolution_convert_fusion = bf16[384,3072]{1,0:T(8,128)(2,1)} fusion(bf16[1536,3072]{0,1:T(8,128)(2,1)} %all-gather.14.cloned.1.call-done, bf16[384,3072]{1,0:T(8,128)(2,1)} %fusion.5, bf16[3072,1536]{1,0:T(8,128)(2,1)} %all-gather.12.cloned.1.call-done), kind=kOutput, calls=%fused_computation.10 | convolution fusion | flops 7254245376 | bytes 23592960 | tf_op jit(solution)/shard_map/dot_general | solution.py:139
  428.9 37.9 %reduce-scatter.2.cloned.1.call-done = bf16[48,3072]{1,0:T(8,128)(2,1)} async-done(((bf16[384,3072]{1,0:T(8,128)(2,1)}), bf16[48,3072]{1,0:T(8,128)(2,1)}) %reduce-scatter.2.cloned.1.call-update) | async-done | bytes 294928 | tf_op jit(solution)/shard_map/reduce_scatter | solution.py:143
  466.8 1.8 fusion.37
  469.5 5.2 %collective-permute-start = (f32[24,64]{1,0:T(8,128)S(1)}, f32[24,64]{1,0:T(8,128)S(1)}, u32[]{:S(2)}, u32[]{:S(2)}) collective-permute-start(f32[24,64]{1,0:T(8,128)S(1)} %constant_dynamic-slice_fusion), channel_id=1, source_target_pairs={{0,128},{128,0},{1,129},{129,1},{2,130},{130,2},{3,131},{131,3},{4... | collective-permute-start | bytes 18440 | tf_op jit(solution)/shard_map/ppermute | solution.py:21
  476.0 1.4 fusion.44
  (81 shorter events, 11.6 us)
Async XLA Ops:
  7.2 102.0 %copy-start = (f32[2,8,4,3072]{3,2,1,0:T(4,128)S(1)}, f32[2,8,4,3072]{3,2,1,0:T(4,128)}, u32[]{:S(2)}) copy-start(f32[2,8,4,3072]{3,2,1,0:T(4,128)} %param.23) | copy-start | bytes 2359300
  7.2 142.1 %all-gather.6.cloned.1.call-start = ((), (), s32[]{:S(2)}) async-start(), calls=%async_computation.1 | async-start | bytes 1327104 | tf_op jit(solution)/shard_map/all_gather | solution.py:113
  32.8 9.4 %copy-start.14 = (s32[1,96]{1,0:T(1,128)S(1)}, s32[1,96]{1,0:T(1,128)}, u32[]{:S(2)}) copy-start(s32[1,96]{1,0:T(1,128)} %param.19) | copy-start | bytes 1156
  64.6 11.8 %copy-start.15 = (s32[8]{0:T(128)S(1)}, s32[8]{0:T(128)}, u32[]{:S(2)}) copy-start(s32[8]{0:T(128)} %param.21) | copy-start | bytes 100
  64.6 13.0 %copy-start.10 = (bf16[1,1,48,1536]{3,2,1,0:T(8,128)(2,1)S(1)}, bf16[1,1,48,1536]{3,2,1,0:T(8,128)(2,1)}, u32[]{:S(2)}) copy-start(bf16[1,1,48,1536]{3,2,1,0:T(8,128)(2,1)} %param.15) | copy-start | bytes 442372
  77.6 7.9 %copy-start.12 = (pred[768]{0:T(1024)(128)(4,1)}, pred[768]{0:T(1024)(128)(4,1)S(1)}, u32[]{:S(2)}) copy-start(pred[768]{0:T(1024)(128)(4,1)S(1)} %iota_compare_fusion) | copy-start | bytes 2308
  83.9 1.8 copy-start.3
  83.9 1.8 copy-start.6
  86.3 1.3 copy-start.4
  92.9 11.9 %copy-start.11 = (f32[12,48]{1,0:T(8,128)S(1)}, f32[12,48]{1,0:T(8,128)}, u32[]{:S(2)}) copy-start(f32[12,48]{1,0:T(8,128)} %fusion.28) | copy-start | bytes 6916
  92.9 11.9 %copy-start.5 = (f32[12,768,48]{1,2,0:T(8,128)S(1)}, f32[12,768,48]{1,2,0:T(8,128)}, u32[]{:S(2)}) copy-start(f32[12,768,48]{1,2,0:T(8,128)} %copy-done.4) | copy-start | bytes 5308420
  92.9 11.9 %copy-start.9 = (f32[48,12,128]{2,0,1:T(8,128)S(1)}, f32[48,12,128]{2,0,1:T(8,128)}, u32[]{:S(2)}) copy-start(f32[48,12,128]{2,0,1:T(8,128)} %convolution_bitcast_fusion.1) | copy-start | bytes 884740
  92.9 11.9 %copy-start.13 = (pred[768]{0:T(1024)(128)(4,1)S(1)}, pred[768]{0:T(1024)(128)(4,1)}, u32[]{:S(2)}) copy-start(pred[768]{0:T(1024)(128)(4,1)} %copy-done.12) | copy-start | bytes 2308
  107.5 93.9 %copy-start.8 = (bf16[1,8,48,384]{3,2,1,0:T(8,128)(2,1)S(1)}, bf16[1,8,48,384]{3,2,1,0:T(8,128)(2,1)}, u32[]{:S(2)}) copy-start(bf16[1,8,48,384]{3,2,1,0:T(8,128)(2,1)} %param.22) | copy-start | bytes 884740
  108.2 93.2 %all-gather.8.cloned.1.call-start = ((), (), s32[]{:S(2)}) async-start(), calls=%async_computation.2 | async-start | bytes 1253376 | tf_op jit(solution)/shard_map/all_gather | solution.py:91
  108.9 135.6 %all-gather.10.cloned.1.call-start = ((), (), s32[]{:S(2)}) async-start(), calls=%async_computation.3 | async-start | bytes 2654208 | tf_op jit(solution)/shard_map/all_gather | solution.py:125
  204.6 124.6 %all-gather.12.cloned.1.call-start = ((), (), s32[]{:S(2)}) async-start(), calls=%async_computation.4 | async-start | bytes 10027008 | tf_op jit(solution)/shard_map/all_gather | solution.py:92
  205.1 206.8 %all-gather.14.cloned.1.call-start = ((), (), s32[]{:S(2)}) async-start(), calls=%async_computation.5 | async-start | bytes 10027008 | tf_op jit(solution)/shard_map/all_gather | solution.py:93
  205.7 261.1 %reduce-scatter.2.cloned.1.call-start = ((), (), s32[]{:S(2)}) async-start(), calls=%async_computation.6 | async-start | bytes 2654208 | tf_op jit(solution)/shard_map/reduce_scatter | solution.py:143
  244.5 2.4 copy-start.2
  412.0 65.5 %copy-start.1 = (f32[2,8,4,3072]{3,2,1,0:T(4,128)S(1)}, f32[2,8,4,3072]{3,2,1,0:T(4,128)}, u32[]{:S(2)}) copy-start(f32[2,8,4,3072]{3,2,1,0:T(4,128)} %param.23) | copy-start | bytes 2359300
  428.1 38.7 %copy-start.7 = (bf16[3072,64]{0,1:T(8,128)(2,1)S(1)}, bf16[3072,64]{0,1:T(8,128)(2,1)}, u32[]{:S(2)}) copy-start(bf16[3072,64]{0,1:T(8,128)(2,1)} %param.27) | copy-start | bytes 1179652
  469.5 6.5 %collective-permute-start = (f32[24,64]{1,0:T(8,128)S(1)}, f32[24,64]{1,0:T(8,128)S(1)}, u32[]{:S(2)}, u32[]{:S(2)}) collective-permute-start(f32[24,64]{1,0:T(8,128)S(1)} %constant_dynamic-slice_fusion), channel_id=1, source_target_pairs={{0,128},{128,0},{1,129},{129,1},{2,130},{130,2},{3,131},{131,3},{4... | collective-permute-start | bytes 18440 | tf_op jit(solution)/shard_map/ppermute | solution.py:21
Sparse Core Ops, SparseCore 0:
  108.3 40.9 all-gather.5
  151.8 49.5 all-gather.7
  204.7 39.7 all-gather.9
  246.8 82.3 all-gather.11
  331.5 80.4 all-gather.13
  428.3 38.5 reduce-scatter.1
where the time goes:
time: 486 us; the launch traced here: 484 us
  waiting for transfers between devices  331 us (68%)
  local copies, waits for them, and re-layouts  71.1 us (15%)
  matrix products  27.3 us (6%)
  blocking collectives  20.3 us (4%)
  between operations  15.2 us (3%)
  other arithmetic  13.6 us (3%)
  starting transfers between devices  5.61 us (1%)
    all_gather x1, waiting for transfers between devices, per_device(): lax.all_gather(down_weight, 'seq', axis=1, tiled=True)  82.8 us
    all_gather x1, waiting for transfers between devices, per_device(): lax.all_gather(up_weight, 'seq', axis=0, tiled=True)  78.9 us
    all_gather x1, waiting for transfers between devices, per_device(): lax.all_gather(out_weight, 'seq', axis=0, tiled=True)  52 us
    all_gather x1, waiting for transfers between devices, per_device(): lax.all_gather(attended, 'req', axis=0, tiled=True)  39.1 us
    all_gather x1, waiting for transfers between devices, per_device(): lax.all_gather(residual.reshape(requests * row_count, col_count), 'req',...  38.7 us
    reduce_scatter x1, waiting for transfers between devices, per_device(): lax.psum_scatter(rows_product(activated, down_rows).astype(jnp.bfloat16),...  37.9 us
    slice x2, local copies, waits for them, and re-layouts, per_device(): image_kv[1]  22.5 us
    all_gather x1, blocking collectives, per_device(): lax.all_gather(fresh_pair, 'seq', axis=1, tiled=True)  20.3 us
  transfers between devices with their start and end apart: 7, of which 6 were waited for; matrix products, arithmetic and copies ran while one was open for 2% of the time, Pallas kernels for 0%

commit v1 on v0

--- a/solution.py
+++ b/solution.py
@@ -9,6 +9,19 @@
 SHIFT = 3.0
 SCALE = 1.0 / math.sqrt(128.0)
 EPSILON = 1e-06
+
+
+def collect(shard, axis, dim):
+    ways = lax.axis_size(axis)
+    up = [(d, (d + 1) % ways) for d in range(ways)]
+    down = [(d, (d - 1) % ways) for d in range(ways)]
+    earlier, later = ([shard], [shard])
+    for _ in range(ways // 2):
+        earlier.append(lax.ppermute(earlier[-1], axis, up))
+    for _ in range((ways - 1) // 2):
+        later.append(lax.ppermute(later[-1], axis, down))
+    line = jnp.concatenate([*earlier[::-1], *later[1:]], axis=dim)
+    return jnp.roll(line, (lax.axis_index(axis) - ways // 2) * shard.shape[dim], axis=dim)
 
 
 def swapped(block, axis, stride):
@@ -122,9 +135,7 @@
         stream[0].astype(jnp.float32)
         + gate_cols[:, None, :] * projected.reshape(requests, row_count, col_count)
     ).astype(jnp.bfloat16)
-    full_rows = lax.all_gather(
-        residual.reshape(requests * row_count, col_count), "req", axis=1, tiled=True
-    )
+    full_rows = collect(residual.reshape(requests * row_count, col_count), "req", 1)
     wide = full_rows.reshape(requests, row_count, -1).astype(jnp.float32)
     average = jnp.mean(wide, axis=-1, keepdims=True)
     centered = wide - average

time: 486 us -> 449 us (0.924)
  waiting for transfers between devices: 331 us -> 263 us
  local copies, waits for them, and re-layouts: 71.1 us -> 91.4 us
  starting transfers between devices: 5.61 us -> 14.9 us
  matrix products: 27.3 us -> 34.3 us
  other arithmetic: 13.6 us -> 8.18 us
    all_gather x1, waiting for transfers between devices: 82.8 us -> 29.7 us  [per_device(): lax.all_gather(down_weight, 'seq', axis=1, tiled=True)]
    all_gather x1 -> x0, waiting for transfers between devices: 38.7 us -> none  [per_device(): lax.all_gather(residual.reshape(requests * row_count, col_count), 'req',...]
    unnamed x6, waiting for transfers between devices: 1.8 us -> 40.4 us
    reduce_scatter x1 -> x0, waiting for transfers between devices: 37.9 us -> none  [per_device(): lax.psum_scatter(rows_product(activated, down_rows).astype(jnp.bfloat16),...]
    ppermute x0 -> x7, waiting for transfers between devices: none -> 20.1 us  [the longest x4 16.9 us: collect(): earlier.append(lax.ppermute(earlier[-1], axis, up))]
    ppermute x0 -> x7, starting transfers between devices: none -> 9.38 us  [the longest x3 8.02 us: collect(): later.append(lax.ppermute(later[-1], axis, down))]
    add x0 -> x2, local copies, waits for them, and re-layouts: none -> 8.83 us  [per_device(): centered * lax.rsqrt(spread + EPSILON) * (1.0 + mod_half[:, 2][:, None, :])]
    mul x0 -> x2, local copies, waits for them, and re-layouts: none -> 8.82 us  [per_device(): centered * lax.rsqrt(spread + EPSILON) * (1.0 + mod_half[:, 2][:, None, :])]
  transfers between devices with their start and end apart: 7 -> 13, of which waited for: 6 -> 9; matrix products, arithmetic and copies ran while one was open for 2% -> 5% of each run, Pallas kernels for 0% -> 0%
where the time goes in v1:
time: 449 us; the launch traced here: 447 us
  waiting for transfers between devices  263 us (59%)
  local copies, waits for them, and re-layouts  91.4 us (20%)
  matrix products  34.3 us (8%)
  blocking collectives  20.3 us (5%)
  between operations  15.1 us (3%)
  starting transfers between devices  14.9 us (3%)
  other arithmetic  8.18 us (2%)
    all_gather x1, waiting for transfers between devices, per_device(): lax.all_gather(up_weight, 'seq', axis=0, tiled=True)  82.8 us
    all_gather x1, waiting for transfers between devices, per_device(): lax.all_gather(out_weight, 'seq', axis=0, tiled=True)  52 us
    unnamed x6, waiting for transfers between devices  40.4 us
    all_gather x1, waiting for transfers between devices, per_device(): lax.all_gather(attended, 'req', axis=0, tiled=True)  37.8 us
    all_gather x1, waiting for transfers between devices, per_device(): lax.all_gather(down_weight, 'seq', axis=1, tiled=True)  29.7 us
    slice x2, local copies, waits for them, and re-layouts, per_device(): image_kv[1]  22.7 us
    dot_general x1, matrix products, rows_product(): return jnp.dot(left_rows, right, preferred_element_type=jnp.float32)  21.5 us
    all_gather x1, blocking collectives, per_device(): lax.all_gather(fresh_pair, 'seq', axis=1, tiled=True)  20.3 us
  transfers between devices with their start and end apart: 13, of which 9 were waited for; matrix products, arithmetic and copies ran while one was open for 5% of the time, Pallas kernels for 0%

profile of v1, /device:TPU:1, one launch (start us, length us, event | category | flops | bytes accessed | tf_op | source)
XLA Modules:
  0.0 447.1 jit_solution(14605338594061725051)
XLA Ops:
  12.5 20.3 %all_gather.15 = bf16[2,96,1536]{2,0,1:T(2,128)(2,1)S(1)} all-gather(bf16[2,6,1536]{2,0,1:T(2,128)(2,1)S(1)} %pad_maximum_fusion.1), channel_id=1, replica_groups=mesh['cfg'=2,'req'=8,'seq'=16] {'seq'}, dimensions={1}, use_global_device_ids=true | all-gather | bytes 626688 | tf_op jit(solution)/shard_map/all_gather | solution.py:103
  32.8 9.4 %copy.122 = bf16[1,1,2,768,1536]{4,2,3,1,0:T(2,128)(2,1)} copy(bf16[1,1,2,768,1536]{4,3,2,1,0:T(8,128)(2,1)} %param.17) | data formatting | bytes 9437184 | tf_op args[2]
  42.2 11.7 %scatter_fusion = bf16[2,768,1536]{2,0,1:T(2,128)(2,1)} fusion(bf16[2,768,1536]{2,0,1:T(2,128)(2,1)} %bitcast.90, s32[96]{0:T(128)S(1)} %fusion.51, bf16[96,2,1536]{2,1,0:T(2,128)(2,1)S(1)} %bitcast.99), kind=kCustom, calls=%fused_computation | custom fusion | bytes 1769856 | tf_op jit(solution)/shard_map/scatter | solution.py:108
  53.9 10.8 %fusion.60 = (bf16[1,768,1536]{2,0,1:T(2,128)(2,1)}, bf16[1,768,1536]{2,0,1:T(2,128)(2,1)}) fusion(bf16[2,768,1536]{2,0,1:T(2,128)(2,1)} %scatter_fusion), kind=kLoop, calls=%fused_computation.117 | loop fusion | bytes 9437184 | tf_op jit(solution)/shard_map/slice | solution.py:120
  64.7 11.8 %copy.85 = bf16[1,768,1536]{1,2,0:T(8,128)(2,1)} copy(bf16[1,768,1536]{2,0,1:T(2,128)(2,1)} %get-tuple-element.3) | data formatting | bytes 4718592 | tf_op jit(solution)/shard_map/slice | solution.py:114
  78.7 3.8 fusion.61
  82.4 1.7 copy.104
  85.5 2.4 bitcast_reduce_fusion
  91.4 1.7 copy.107
  94.5 11.9 %copy.90 = bf16[1,768,1536]{1,2,0:T(8,128)(2,1)} copy(bf16[1,768,1536]{2,0,1:T(2,128)(2,1)} %get-tuple-element.2) | data formatting | bytes 4718592 | tf_op jit(solution)/shard_map/slice | solution.py:120
  106.5 2.7 fusion.29
  113.2 37.8 %all-gather.5.cloned.1.call-done = bf16[384,1536]{1,0:T(8,128)(2,1)} async-done(((bf16[48,1536]{1,0:T(8,128)(2,1)}), bf16[384,1536]{1,0:T(8,128)(2,1)}) %all-gather.5.cloned.1.call-update) | async-done | bytes 1179664 | tf_op jit(solution)/shard_map/all_gather | solution.py:126
  151.0 52.0 %all-gather.7.cloned.1.call-done = bf16[1536,384]{1,0:T(8,128)(2,1)} async-done(((bf16[96,384]{1,0:T(8,128)(2,1)}), bf16[1536,384]{1,0:T(8,128)(2,1)}) %all-gather.7.cloned.1.call-update) | async-done | bytes 1179664 | tf_op jit(solution)/shard_map/all_gather | solution.py:104
  203.1 2.4 fusion.25
  206.9 7.5 %collective-permute-done = bf16[384,384]{0,1:T(8,128)(2,1)S(1)} collective-permute-done((bf16[384,384]{0,1:T(8,128)(2,1)S(1)}, bf16[384,384]{0,1:T(8,128)(2,1)S(1)}, u32[]{:S(2)}, u32[]{:S(2)}) %collective-permute-start) | collective-permute-done | bytes 294944 | tf_op jit(solution)/shard_map/ppermute | solution.py:20
  214.4 2.7 collective-permute-start.4
  217.1 4.8 %collective-permute-done.1 = bf16[384,384]{0,1:T(8,128)(2,1)S(1)} collective-permute-done((bf16[384,384]{0,1:T(8,128)(2,1)S(1)}, bf16[384,384]{0,1:T(8,128)(2,1)S(1)}, u32[]{:S(2)}, u32[]{:S(2)}) %collective-permute-start.1) | collective-permute-done | bytes 294944 | tf_op jit(solution)/shard_map/ppermute | solution.py:20
  221.9 2.7 collective-permute-start.5
  224.6 4.5 %collective-permute-done.2 = bf16[384,384]{0,1:T(8,128)(2,1)S(1)} collective-permute-done((bf16[384,384]{0,1:T(8,128)(2,1)S(1)}, bf16[384,384]{0,1:T(8,128)(2,1)S(1)}, u32[]{:S(2)}, u32[]{:S(2)}) %collective-permute-start.2) | collective-permute-done | bytes 294944 | tf_op jit(solution)/shard_map/ppermute | solution.py:20
  229.1 2.8 mul.275
  231.8 6.1 %copy.95 = f32[384,3072]{0,1:T(8,128)} copy(f32[384,3072]{1,0:T(8,128)} %bitcast.91) | data formatting | bytes 9437184 | tf_op jit(solution)/shard_map/mul | solution.py:144
  237.9 2.8 add.179
  240.7 6.1 %copy.96 = f32[384,3072]{0,1:T(8,128)} copy(f32[384,3072]{1,0:T(8,128)} %bitcast.92) | data formatting | bytes 9437184 | tf_op jit(solution)/shard_map/add | solution.py:144
  246.7 2.7 collective-permute-start.6
  249.8 3.3 collective-permute-done.6
  254.3 1.5 copy-done.4
  256.8 29.7 %all-gather.11.cloned.1.call-done = bf16[1536,3072]{0,1:T(8,128)(2,1)} async-done(((bf16[1536,192]{0,1:T(8,128)(2,1)}), bf16[1536,3072]{0,1:T(8,128)(2,1)}) %all-gather.11.cloned.1.call-update) | async-done | bytes 9437200 | tf_op jit(solution)/shard_map/all_gather | solution.py:106
  286.5 82.8 %all-gather.9.cloned.1.call-done = bf16[3072,1536]{1,0:T(8,128)(2,1)} async-done(((bf16[192,1536]{1,0:T(8,128)(2,1)}), bf16[3072,1536]{1,0:T(8,128)(2,1)}) %all-gather.9.cloned.1.call-update) | async-done | bytes 9437200 | tf_op jit(solution)/shard_map/all_gather | solution.py:105
  369.3 21.5 %convolution_convert_fusion = bf16[384,3072]{1,0:T(8,128)(2,1)} fusion(bf16[1536,3072]{0,1:T(8,128)(2,1)} %all-gather.11.cloned.1.call-done, bf16[3072,1536]{1,0:T(8,128)(2,1)} %all-gather.9.cloned.1.call-done, f32[384,3072]{0,1:T(8,128)} %copy.96, f32[384,3072]{0,1:T(8,128)} %copy.95, f32[384]{0:T(512)S(1)} %add_rsqrt_fusion, ...), kind=kOutput, calls=%fused_computation.10 | convolution fusion | flops 7261323264 | bytes 33033220 | tf_op jit(solution)/shard_map/dot_general | solution.py:150
  390.9 38.5 %reduce-scatter.4.cloned.1.call-done = bf16[48,3072]{1,0:T(8,128)(2,1)} async-done(((bf16[384,3072]{1,0:T(8,128)(2,1)}), bf16[48,3072]{1,0:T(8,128)(2,1)}) %reduce-scatter.4.cloned.1.call-update) | async-done | bytes 294928
  430.8 2.4 fusion.37
  433.4 5.1 %collective-permute-start.7 = (f32[24,64]{1,0:T(8,128)S(1)}, f32[24,64]{1,0:T(8,128)S(1)}, u32[]{:S(2)}, u32[]{:S(2)}) collective-permute-start(f32[24,64]{1,0:T(8,128)S(1)} %constant_dynamic-slice_fusion), channel_id=1, source_target_pairs={{0,128},{128,0},{1,129},{129,1},{2,130},{130,2},{3,131},{131,3},{4... | collective-permute-start | bytes 18440 | tf_op jit(solution)/shard_map/ppermute | solution.py:34
  (112 shorter events, 24.2 us)
Async XLA Ops:
  7.2 105.1 %copy-start = (f32[2,8,4,3072]{3,2,1,0:T(4,128)S(1)}, f32[2,8,4,3072]{3,2,1,0:T(4,128)}, u32[]{:S(2)}) copy-start(f32[2,8,4,3072]{3,2,1,0:T(4,128)} %param.23) | copy-start | bytes 2359300
  7.2 143.9 %all-gather.5.cloned.1.call-start = ((), (), s32[]{:S(2)}) async-start(), calls=%async_computation.1 | async-start | bytes 1327104 | tf_op jit(solution)/shard_map/all_gather | solution.py:126
  32.8 9.4 %copy-start.13 = (s32[1,96]{1,0:T(1,128)S(1)}, s32[1,96]{1,0:T(1,128)}, u32[]{:S(2)}) copy-start(s32[1,96]{1,0:T(1,128)} %param.19) | copy-start | bytes 1156
  64.7 11.8 %copy-start.14 = (s32[8]{0:T(128)S(1)}, s32[8]{0:T(128)}, u32[]{:S(2)}) copy-start(s32[8]{0:T(128)} %param.21) | copy-start | bytes 100
  64.7 13.1 %copy-start.7 = (bf16[1,1,48,1536]{3,2,1,0:T(8,128)(2,1)S(1)}, bf16[1,1,48,1536]{3,2,1,0:T(8,128)(2,1)}, u32[]{:S(2)}) copy-start(bf16[1,1,48,1536]{3,2,1,0:T(8,128)(2,1)} %param.15) | copy-start | bytes 442372
  77.8 7.7 %copy-start.10 = (pred[768]{0:T(1024)(128)(4,1)}, pred[768]{0:T(1024)(128)(4,1)S(1)}, u32[]{:S(2)}) copy-start(pred[768]{0:T(1024)(128)(4,1)S(1)} %iota_compare_fusion) | copy-start | bytes 2308
  87.9 1.3 copy-start.2
  94.5 11.9 %copy-start.8 = (f32[12,48]{1,0:T(8,128)S(1)}, f32[12,48]{1,0:T(8,128)}, u32[]{:S(2)}) copy-start(f32[12,48]{1,0:T(8,128)} %fusion.30) | copy-start | bytes 6916
  94.5 11.9 %copy-start.3 = (f32[12,768,48]{1,2,0:T(8,128)S(1)}, f32[12,768,48]{1,2,0:T(8,128)}, u32[]{:S(2)}) copy-start(f32[12,768,48]{1,2,0:T(8,128)} %copy-done.2) | copy-start | bytes 5308420
  94.5 11.9 %copy-start.5 = (f32[48,12,128]{2,0,1:T(8,128)S(1)}, f32[48,12,128]{2,0,1:T(8,128)}, u32[]{:S(2)}) copy-start(f32[48,12,128]{2,0,1:T(8,128)} %convolution_bitcast_fusion.1) | copy-start | bytes 884740
  94.5 11.9 %copy-start.11 = (pred[768]{0:T(1024)(128)(4,1)S(1)}, pred[768]{0:T(1024)(128)(4,1)}, u32[]{:S(2)}) copy-start(pred[768]{0:T(1024)(128)(4,1)} %copy-done.10) | copy-start | bytes 2308
  106.5 6.4 %copy-start.6 = (bf16[1,8,48,384]{3,2,1,0:T(8,128)(2,1)S(1)}, bf16[1,8,48,384]{3,2,1,0:T(8,128)(2,1)}, u32[]{:S(2)}) copy-start(bf16[1,8,48,384]{3,2,1,0:T(8,128)(2,1)} %param.22) | copy-start | bytes 884740
  109.9 93.1 %all-gather.7.cloned.1.call-start = ((), (), s32[]{:S(2)}) async-start(), calls=%async_computation.2 | async-start | bytes 1253376 | tf_op jit(solution)/shard_map/all_gather | solution.py:104
  110.7 175.9 %all-gather.11.cloned.1.call-start = ((), (), s32[]{:S(2)}) async-start(), calls=%async_computation.4 | async-start | bytes 10027008 | tf_op jit(solution)/shard_map/all_gather | solution.py:106
  111.4 257.9 %all-gather.9.cloned.1.call-start = ((), (), s32[]{:S(2)}) async-start(), calls=%async_computation.3 | async-start | bytes 10027008 | tf_op jit(solution)/shard_map/all_gather | solution.py:105
  112.0 317.5 %reduce-scatter.4.cloned.1.call-start = ((), (), s32[]{:S(2)}) async-start(), calls=%async_computation.5 | async-start | bytes 2654208
  205.5 8.9 %collective-permute-start = (bf16[384,384]{0,1:T(8,128)(2,1)S(1)}, bf16[384,384]{0,1:T(8,128)(2,1)S(1)}, u32[]{:S(2)}, u32[]{:S(2)}) collective-permute-start(bf16[384,384]{0,1:T(8,128)(2,1)S(1)} %fusion.25), channel_id=1, source_target_pairs={{0,16},{16,32},{32,48},{48,64},{64,80},{80,96},{96,112},{112,0},{1... | collective-permute-start | bytes 884744 | tf_op jit(solution)/shard_map/ppermute | solution.py:20
  214.4 7.5 %collective-permute-start.1 = (bf16[384,384]{0,1:T(8,128)(2,1)S(1)}, bf16[384,384]{0,1:T(8,128)(2,1)S(1)}, u32[]{:S(2)}, u32[]{:S(2)}) collective-permute-start(bf16[384,384]{0,1:T(8,128)(2,1)S(1)} %collective-permute-done), channel_id=1, source_target_pairs={{0,16},{16,32},{32,48},{48,64},{64,80},{80,96},{96,112},{112,0},{1... | collective-permute-start | bytes 884744 | tf_op jit(solution)/shard_map/ppermute | solution.py:20
  214.4 7.5 %collective-permute-start.4 = (bf16[384,384]{0,1:T(8,128)(2,1)S(1)}, bf16[384,384]{0,1:T(8,128)(2,1)S(1)}, u32[]{:S(2)}, u32[]{:S(2)}) collective-permute-start(bf16[384,384]{0,1:T(8,128)(2,1)S(1)} %fusion.25), channel_id=1, source_target_pairs={{0,112},{16,0},{32,16},{48,32},{64,48},{80,64},{96,80},{112,96},{1... | collective-permute-start | bytes 884744 | tf_op jit(solution)/shard_map/ppermute | solution.py:22
  221.9 7.2 %collective-permute-start.2 = (bf16[384,384]{0,1:T(8,128)(2,1)S(1)}, bf16[384,384]{0,1:T(8,128)(2,1)S(1)}, u32[]{:S(2)}, u32[]{:S(2)}) collective-permute-start(bf16[384,384]{0,1:T(8,128)(2,1)S(1)} %collective-permute-done.1), channel_id=1, source_target_pairs={{0,16},{16,32},{32,48},{48,64},{64,80},{80,96},{96,112},{112,0},{1... | collective-permute-start | bytes 884744 | tf_op jit(solution)/shard_map/ppermute | solution.py:20
  221.9 24.8 %collective-permute-start.5 = (bf16[384,384]{0,1:T(8,128)(2,1)S(1)}, bf16[384,384]{0,1:T(8,128)(2,1)S(1)}, u32[]{:S(2)}, u32[]{:S(2)}) collective-permute-start(bf16[384,384]{0,1:T(8,128)(2,1)S(1)} %collective-permute-done.4), channel_id=1, source_target_pairs={{0,112},{16,0},{32,16},{48,32},{64,48},{80,64},{96,80},{112,96},{1... | collective-permute-start | bytes 884744 | tf_op jit(solution)/shard_map/ppermute | solution.py:22
  229.1 20.3 %collective-permute-start.3 = (bf16[384,384]{0,1:T(8,128)(2,1)S(1)}, bf16[384,384]{0,1:T(8,128)(2,1)S(1)}, u32[]{:S(2)}, u32[]{:S(2)}) collective-permute-start(bf16[384,384]{0,1:T(8,128)(2,1)S(1)} %collective-permute-done.2), channel_id=1, source_target_pairs={{0,16},{16,32},{32,48},{48,64},{64,80},{80,96},{96,112},{112,0},{1... | collective-permute-start | bytes 884744 | tf_op jit(solution)/shard_map/ppermute | solution.py:20
  246.7 6.3 %collective-permute-start.6 = (bf16[384,384]{0,1:T(8,128)(2,1)S(1)}, bf16[384,384]{0,1:T(8,128)(2,1)S(1)}, u32[]{:S(2)}, u32[]{:S(2)}) collective-permute-start(bf16[384,384]{0,1:T(8,128)(2,1)S(1)} %collective-permute-done.5), channel_id=1, source_target_pairs={{0,112},{16,0},{32,16},{48,32},{64,48},{80,64},{96,80},{112,96},{1... | collective-permute-start | bytes 884744 | tf_op jit(solution)/shard_map/ppermute | solution.py:22
  253.6 2.2 copy-start.4
  256.8 174.0 %copy-start.12 = (bf16[3072,64]{0,1:T(8,128)(2,1)S(1)}, bf16[3072,64]{0,1:T(8,128)(2,1)}, u32[]{:S(2)}) copy-start(bf16[3072,64]{0,1:T(8,128)(2,1)} %param.27) | copy-start | bytes 1179652
  369.3 71.2 %copy-start.1 = (f32[2,8,4,3072]{3,2,1,0:T(4,128)S(1)}, f32[2,8,4,3072]{3,2,1,0:T(4,128)}, u32[]{:S(2)}) copy-start(f32[2,8,4,3072]{3,2,1,0:T(4,128)} %param.23) | copy-start | bytes 2359300
  390.9 49.0 %copy-start.9 = (f32[1,24,64]{2,1,0:T(8,128)S(1)}, f32[1,24,64]{2,1,0:T(8,128)}, u32[]{:S(2)}) copy-start(f32[1,24,64]{2,1,0:T(8,128)} %param.28) | copy-start | bytes 18436
  433.4 6.5 %collective-permute-start.7 = (f32[24,64]{1,0:T(8,128)S(1)}, f32[24,64]{1,0:T(8,128)S(1)}, u32[]{:S(2)}, u32[]{:S(2)}) collective-permute-start(f32[24,64]{1,0:T(8,128)S(1)} %constant_dynamic-slice_fusion), channel_id=1, source_target_pairs={{0,128},{128,0},{1,129},{129,1},{2,130},{130,2},{3,131},{131,3},{4... | collective-permute-start | bytes 18440 | tf_op jit(solution)/shard_map/ppermute | solution.py:34
Sparse Core Ops, SparseCore 0:
  110.0 40.9 all-gather.4
  153.5 49.5 all-gather.6
  205.5 80.9 all-gather.10
  288.8 80.4 all-gather.8
  391.0 38.3 reduce-scatter.3
